TPU v7x, 32 devices: a whole 2x2x4 slice. The times are simulated.
32 devices in a mesh: grp: 1, blk: 32 (over z, y, x, core).
Axes of the slice: x: 2, y: 2, z: 4, core: 2. Of those that a mesh axis runs over, the one named last changes fastest.
Arguments:
- activations: bfloat16 [4096, 8192], P(('grp', 'blk')), may hold values from -6 to 6
- out_grads: bfloat16 [4096, 28672], P(('grp', 'blk')), may hold values from -6 to 6
- query_factors: bfloat16 [384, 36864], P('blk'), may hold values from -0.046875 to 0.046875
- pair_query: int32 [384], replicated, may hold values from 0 to 11, as said below
- segment_ids: int32 [4096], P(('grp', 'blk')), may hold values from 0 to 3, never falling along the last dimension, each value on 1 to 2048 neighbouring positions
Outputs:
- token_scores: float32 [4096, 12], P(('grp', 'blk'))
- seq_scores: float32 [4, 12], P('grp')
Inputs may be any that keep to these rules, and one draw needn't show every extreme that they name: `pair_query`: each query id appears exactly 32 times. `segment_ids`: never falling; each sequence has 1 to 2048 tokens, one exactly 2048.
All inputs are finite; a program needn't handle non-finite values.
Results may differ from a plain program's by a relative error of at most 0.0003.
Values may be sent and summed in bfloat16 or wider, within the bound.
A program may use at most 192 MiB of HBM per device.

v0:
```python
import jax
import jax.numpy as jnp
from jax import lax
from jax.sharding import PartitionSpec as P

QUERIES = 12
SEQ_LEN = 2048


def pair_products(activations, out_grads, piece):
    width = out_grads.shape[1]
    numbers = (((1,), (1,)), ((), ()))
    out_proj = lax.dot_general(
        out_grads, piece[:, :width], numbers, preferred_element_type=jnp.float32
    )
    in_proj = lax.dot_general(
        activations, piece[:, width:], numbers, preferred_element_type=jnp.float32
    )
    return out_proj * in_proj


def local(activations, out_grads, query_factors, pair_query, segment_ids):
    owner = (pair_query[:, None] == jnp.arange(QUERIES, dtype=jnp.int32)[None, :]).astype(
        jnp.float32
    )
    contrib = pair_products(
        activations, out_grads, lax.all_gather(query_factors, "blk", axis=0, tiled=True)
    )
    token_scores = jnp.dot(contrib, owner, precision=lax.Precision.HIGHEST)
    seq_total = 2 * activations.shape[0] * lax.axis_size("blk") // SEQ_LEN
    member = (segment_ids[:, None] == jnp.arange(seq_total, dtype=jnp.int32)[None, :]).astype(
        jnp.float32
    )
    partial_sums = jnp.dot(member.T, token_scores, precision=lax.Precision.HIGHEST)
    partial_counts = jnp.sum(member, axis=0)
    totals, counts = lax.psum((partial_sums, partial_counts), "blk")
    seq_scores = totals / jnp.sqrt(counts)[:, None]
    return (token_scores, seq_scores)


def solution(mesh):
    in_specs = (
        P(("grp", "blk"), None),
        P(("grp", "blk"), None),
        P("blk", None),
        P(),
        P(("grp", "blk")),
    )
    out_specs = (P(("grp", "blk"), None), P("grp", None))
    return jax.shard_map(local, mesh=mesh, in_specs=in_specs, out_specs=out_specs, check_vma=False)
```

profile of v0, /device:TPU:0, one launch (start us, length us, event | category | flops | bytes accessed | tf_op | source)
XLA Modules:
  0.0 319.9 jit_solution(5725825209001183801)
XLA Ops:
  7.2 0.0 copy-start
  7.2 0.0 all-gather.3.cloned.1.call-start
  7.2 0.7 all-gather.3.cloned.1.call-update
  7.9 0.8 convert_reduce_fusion
  8.7 219.3 %all-gather.3.cloned.1.call-done = bf16[32,12,36864]{2,1,0:T(8,128)(2,1)} async-done(((bf16[1,12,36864]{2,1,0:T(8,128)(2,1)}), bf16[32,12,36864]{2,1,0:T(8,128)(2,1)}) %all-gather.3.cloned.1.call-update) | async-done | bytes 28311568 | tf_op jit(solution)/shard_map/all_gather | solution.py:27
  228.0 28.2 %reshape.8 = bf16[384,36864]{1,0:T(8,128)(2,1)} reshape(bf16[32,12,36864]{2,1,0:T(8,128)(2,1)} %all-gather.3.cloned.1.call-done) | data formatting | bytes 56623104
  256.2 12.5 %fusion = f32[128,384]{1,0:T(8,128)S(1)} fusion(bf16[128,28672]{1,0:T(8,128)(2,1)} %param.6, bf16[384,36864]{1,0:T(8,128)(2,1)} %reshape.8), kind=kOutput, calls=%fused_computation | convolution fusion | flops 2818572288 | bytes 29556736 | tf_op jit(solution)/shard_map/dot_general | solution.py:13
  268.7 0.0 copy-done
  268.7 0.0 copy-start.2
  268.7 0.0 copy-start.3
  268.7 4.8 %fusion.4 = f32[128,384]{1,0:T(8,128)S(1)} fusion(f32[128,384]{1,0:T(8,128)S(1)} %fusion, bf16[128,8192]{1,0:T(8,128)(2,1)S(1)} %copy-done, bf16[384,36864]{1,0:T(8,128)(2,1)} %reshape.8), kind=kOutput, calls=%fused_computation.4 | convolution fusion | flops 805355520 | bytes 8781824 | tf_op jit(solution)/shard_map/dot_general | solution.py:16
  273.5 0.0 copy-done.2
  273.5 0.4 fusion.7
  273.9 0.0 copy-done.3
  273.9 0.0 copy-start.1
  273.9 0.1 fusion.9
  274.0 38.3 %all-reduce = (f32[4,12]{1,0:T(4,128)S(1)}, f32[4]{0:T(128)S(1)}) all-reduce(f32[4,12]{1,0:T(4,128)S(1)} %fusion.9, f32[4]{0:T(128)S(1)} %convert_reduce_fusion), channel_id=1, replica_groups=mesh['grp'=1,'blk'=32] {'blk'}, use_global_device_ids=true, to_apply=%region_0.0 | all-reduce | flops 52 | bytes 416 | tf_op jit(solution)/shard_map/psum | solution.py:36
  312.3 0.7 broadcast_divide_fusion
  313.0 0.0 copy-done.1
  (1 shorter events, 0.0 us)
Async XLA Ops:
  7.2 261.5 %copy-start = (bf16[128,8192]{1,0:T(8,128)(2,1)S(1)}, bf16[128,8192]{1,0:T(8,128)(2,1)}, u32[]{:S(2)}) copy-start(bf16[128,8192]{1,0:T(8,128)(2,1)} %param.5) | copy-start | bytes 6291460
  7.2 220.8 %all-gather.3.cloned.1.call-start = ((), (), s32[]{:S(2)}) async-start(), calls=%async_computation | async-start | bytes 38928384 | tf_op jit(solution)/shard_map/all_gather | solution.py:27
  268.7 4.8 %copy-start.2 = (s32[384]{0:T(512)S(1)}, s32[384]{0:T(512)}, u32[]{:S(2)}) copy-start(s32[384]{0:T(512)} %param.8) | copy-start | bytes 4612
  268.7 5.2 %copy-start.3 = (s32[128]{0:T(128)S(1)}, s32[128]{0:T(128)}, u32[]{:S(2)}) copy-start(s32[128]{0:T(128)} %param.9) | copy-start | bytes 1540
  273.9 39.1 %copy-start.1 = (f32[128,12]{0,1:T(8,128)}, f32[128,12]{0,1:T(8,128)S(1)}, u32[]{:S(2)}) copy-start(f32[128,12]{0,1:T(8,128)S(1)} %fusion.7) | copy-start | bytes 18436
Sparse Core Ops, SparseCore 0:
  10.9 217.0 all-gather.2
where the time goes:
time: 320 us
  waiting for transfers between devices  220 us (69%)
  blocking collectives  38.3 us (12%)
  local copies, waits for them, and re-layouts  28.2 us (9%)
  matrix products  17.8 us (6%)
  between operations  14.1 us (4%)
    all_gather x1, waiting for transfers between devices, local(): lax.all_gather(query_factors, 'blk', axis=0, tiled=True)  219 us
    psum x1, blocking collectives, local(): totals, counts = lax.psum((partial_sums, partial_counts), 'blk')  38.3 us
    unnamed x9, local copies, waits for them, and re-layouts  28.2 us
    dot_general x1, matrix products, pair_products(): lax.dot_general(out_grads, piece[:, :width], numbers, preferred_element_t...  12.5 us
  transfers between devices with their start and end apart: 1, of which 1 were waited for; matrix products, arithmetic and copies ran while one was open for 0% of the time, Pallas kernels for 0%

commit v1 on v0

--- a/solution.py
+++ b/solution.py
@@ -20,14 +20,27 @@
 
 
 def local(activations, out_grads, query_factors, pair_query, segment_ids):
-    owner = (pair_query[:, None] == jnp.arange(QUERIES, dtype=jnp.int32)[None, :]).astype(
+    n = lax.axis_size("blk")
+    me = lax.axis_index("blk")
+    core = lax.rem(me, 2)
+    rows = query_factors.shape[0]
+    swap = [(i, i ^ 1) for i in range(n)]
+    groups = [list(range(0, n, 2)), list(range(1, n, 2))]
+    gathered = lax.all_gather(query_factors, "blk", axis=0, tiled=True, axis_index_groups=groups)
+    other_acts = lax.ppermute(activations, "blk", swap)
+    other_grads = lax.ppermute(out_grads, "blk", swap)
+    mine = lax.dynamic_index_in_dim(pair_query.reshape(n // 2, 2, rows), core, axis=1, keepdims=False)
+    owner = (mine.reshape(-1)[:, None] == jnp.arange(QUERIES, dtype=jnp.int32)[None, :]).astype(
         jnp.float32
     )
-    contrib = pair_products(
-        activations, out_grads, lax.all_gather(query_factors, "blk", axis=0, tiled=True)
+    other_part = jnp.dot(
+        pair_products(other_acts, other_grads, gathered), owner, precision=lax.Precision.HIGHEST
     )
-    token_scores = jnp.dot(contrib, owner, precision=lax.Precision.HIGHEST)
-    seq_total = 2 * activations.shape[0] * lax.axis_size("blk") // SEQ_LEN
+    back = lax.ppermute(other_part, "blk", swap)
+    token_scores = back + jnp.dot(
+        pair_products(activations, out_grads, gathered), owner, precision=lax.Precision.HIGHEST
+    )
+    seq_total = 2 * activations.shape[0] * n // SEQ_LEN
     member = (segment_ids[:, None] == jnp.arange(seq_total, dtype=jnp.int32)[None, :]).astype(
         jnp.float32
     )

time: 320 us -> 308 us (0.963)
  local copies, waits for them, and re-layouts: 28.2 us -> 16.1 us
  waiting for transfers between devices: 220 us -> 215 us
  matrix products: 17.8 us -> 21.6 us
    unnamed x9 -> x7, local copies, waits for them, and re-layouts: 28.2 us -> 15.2 us
    all_gather x1, waiting for transfers between devices: 219 us -> 214 us  [local(): lax.all_gather(query_factors, 'blk', axis=0, tiled=True, axis_index_group...]
    dot_general x1 -> x2, matrix products: 12.5 us -> 15.4 us  [pair_products(): lax.dot_general(out_grads, piece[:, :width], numbers, preferred_element_t...]
  transfers between devices with their start and end apart: 1 -> 4, of which waited for: 1 -> 1; matrix products, arithmetic and copies ran while one was open for 0% -> 10% of each run, Pallas kernels for 0% -> 0%
where the time goes in v1:
time: 308 us; the launch traced here: 307 us
  waiting for transfers between devices  215 us (70%)
  blocking collectives  38.3 us (12%)
  matrix products  21.6 us (7%)
  local copies, waits for them, and re-layouts  16.1 us (5%)
  between operations  14.1 us (5%)
    all_gather x1, waiting for transfers between devices, local(): lax.all_gather(query_factors, 'blk', axis=0, tiled=True, axis_index_group...  214 us
    psum x1, blocking collectives, local(): totals, counts = lax.psum((partial_sums, partial_counts), 'blk')  38.3 us
    dot_general x2, matrix products, pair_products(): lax.dot_general(out_grads, piece[:, :width], numbers, preferred_element_t...  15.4 us
    unnamed x7, local copies, waits for them, and re-layouts  15.2 us
  transfers between devices with their start and end apart: 4, of which 1 were waited for; matrix products, arithmetic and copies ran while one was open for 10% of the time, Pallas kernels for 0%

profile of v1, /device:TPU:0, one launch (start us, length us, event | category | flops | bytes accessed | tf_op | source)
XLA Modules:
  0.0 307.2 jit_solution(12985338528874544045)
XLA Ops:
  7.2 0.0 all-gather.3.cloned.1.call-start
  7.2 0.7 all-gather.3.cloned.1.call-update
  7.9 0.6 collective-permute-start
  8.5 0.1 collective-permute-start.1
  8.5 0.8 reshape.11
  9.4 0.1 eq.28
  9.5 0.8 convert_reduce_fusion
  10.2 214.2 %all-gather.3.cloned.1.call-done = bf16[16,12,36864]{2,1,0:T(8,128)(2,1)} async-done(((bf16[1,12,36864]{2,1,0:T(8,128)(2,1)}), bf16[16,12,36864]{2,1,0:T(8,128)(2,1)}) %all-gather.3.cloned.1.call-update) | async-done | bytes 14155792 | tf_op jit(solution)/shard_map/all_gather | solution.py:29
  224.4 14.4 %reshape.13 = bf16[192,36864]{1,0:T(8,128)(2,1)} reshape(bf16[16,12,36864]{2,1,0:T(8,128)(2,1)} %all-gather.3.cloned.1.call-done) | data formatting | bytes 28311552
  238.8 0.0 collective-permute-done.1
  238.8 2.9 fusion.6
  241.7 9.4 %fusion = f32[128,192]{0,1:T(8,128)S(1)} fusion(bf16[128,28672]{1,0:T(8,128)(2,1)} %param.6, bf16[192,36864]{1,0:T(8,128)(2,1)} %reshape.13), kind=kOutput, calls=%fused_computation | convolution fusion | flops 1409286144 | bytes 18448384 | tf_op jit(solution)/shard_map/dot_general | solution.py:13
  251.1 0.0 copy-start.2
  251.1 0.0 collective-permute-done
  251.1 0.8 copy-done
  251.9 6.1 %fusion.11 = f32[128,192]{0,1:T(8,128)S(1)} fusion(f32[128,192]{0,1:T(8,128)S(1)} %fusion.6, bf16[128,28672]{1,0:T(8,128)(2,1)} %collective-permute-done, bf16[192,36864]{1,0:T(8,128)(2,1)S(1)} %copy-done), kind=kOutput, calls=%fused_computation.9 | convolution fusion | flops 1409310720 | bytes 18546688 | tf_op jit(solution)/shard_map/dot_general | solution.py:13
  258.0 0.3 fusion.14
  258.3 0.0 collective-permute-start.2
  258.3 2.6 fusion.8
  260.9 0.0 collective-permute-done.2
  260.9 0.3 convolution_add_fusion
  261.2 0.1 fusion.17
  261.3 38.3 %all-reduce = (f32[4,12]{1,0:T(4,128)S(1)}, f32[4]{0:T(128)S(1)}) all-reduce(f32[4,12]{1,0:T(4,128)S(1)} %fusion.17, f32[4]{0:T(128)S(1)} %convert_reduce_fusion), channel_id=1, replica_groups=mesh['grp'=1,'blk'=32] {'blk'}, use_global_device_ids=true, to_apply=%region_0.1 | all-reduce | flops 52 | bytes 416 | tf_op jit(solution)/shard_map/psum | solution.py:49
  299.7 0.7 broadcast_divide_fusion
  (6 shorter events, 0.0 us)
Async XLA Ops:
  7.2 217.2 %all-gather.3.cloned.1.call-start = ((), (), s32[]{:S(2)}) async-start(), calls=%async_computation | async-start | bytes 20054016 | tf_op jit(solution)/shard_map/all_gather | solution.py:29
  7.9 243.2 %collective-permute-start = (bf16[128,28672]{1,0:T(8,128)(2,1)}, bf16[128,28672]{1,0:T(8,128)(2,1)}, u32[]{:S(2)}, u32[]{:S(2)}) collective-permute-start(bf16[128,28672]{1,0:T(8,128)(2,1)} %param.6), channel_id=1, source_target_pairs={{0,1},{1,0},{2,3},{3,2},{4,5},{5,4},{6,7},{7,6},{8,9},{9,8},{10,11... | collective-permute-start | bytes 22020104 | tf_op jit(solution)/shard_map/ppermute | solution.py:31
  8.5 230.3 %collective-permute-start.1 = (bf16[128,8192]{1,0:T(8,128)(2,1)}, bf16[128,8192]{1,0:T(8,128)(2,1)S(1)}, u32[]{:S(2)}, u32[]{:S(2)}) collective-permute-start(bf16[128,8192]{1,0:T(8,128)(2,1)} %param.5), channel_id=1, source_target_pairs={{0,1},{1,0},{2,3},{3,2},{4,5},{5,4},{6,7},{7,6},{8,9},{9,8},{10,11... | collective-permute-start | bytes 6291464 | tf_op jit(solution)/shard_map/ppermute | solution.py:30
  241.7 10.2 %copy-start = (bf16[192,36864]{1,0:T(8,128)(2,1)S(1)}, bf16[192,36864]{1,0:T(8,128)(2,1)}, u32[]{:S(2)}) copy-start(bf16[192,36864]{1,0:T(8,128)(2,1)} %reshape.13) | copy-start | bytes 42467332
  251.1 10.1 %copy-start.2 = (s32[128]{0:T(128)S(1)}, s32[128]{0:T(128)}, u32[]{:S(2)}) copy-start(s32[128]{0:T(128)} %param.9) | copy-start | bytes 1540
  258.3 2.6 collective-permute-start.2
  261.2 39.1 %copy-start.1 = (f32[128,12]{0,1:T(8,128)}, f32[128,12]{0,1:T(8,128)S(1)}, u32[]{:S(2)}) copy-start(f32[128,12]{0,1:T(8,128)S(1)} %convolution_add_fusion) | copy-start | bytes 18436
Sparse Core Ops, SparseCore 0:
  10.8 213.5 all-gather.2

commit v2 on v1

--- a/solution.py
+++ b/solution.py
@@ -1,6 +1,8 @@
 import jax
 import jax.numpy as jnp
 from jax import lax
+from jax.experimental import pallas as pl
+from jax.experimental.pallas import tpu as pltpu
 from jax.sharding import PartitionSpec as P
 
 QUERIES = 12
@@ -51,7 +53,352 @@
     return (token_scores, seq_scores)
 
 
+MESH = pl.DeviceIdType.MESH
+SUB = 8
+LANES = 128
+CHUNK = 1024
+LAG = 2
+DEPTH_PLANE = 2
+
+
+def depth_of(mesh):
+    sizes = dict(mesh.shape)
+    if sizes.get("grp") != 1 or sizes["blk"] % 8:
+        return 0
+    devices = mesh.devices.reshape(-1)
+    first = devices[0].coords
+    for i, d in enumerate(devices):
+        at = tuple(c - f for c, f in zip(d.coords, first))
+        if at != ((i // 2) % 2, (i // 4) % 2, i // 8) or d.core_on_chip != i % 2:
+            return 0
+    return sizes["blk"] // 8
+
+
+def kernel(nz, kc, seqs, half_out, slabs, acts, grads, ids, owner, ts_out, seq_out,
+           buf, tok_l, tok_r, acc, ids2, part, part_in, sums, plane_in, line, line_in,
+           recv_sem, send_sem, tok_sem, tok_send, own_sem, ids_sem, back_sem, plane_sem, line_sem):
+    me = lax.axis_index("blk")
+    core = lax.rem(me, 2)
+    chip = me // 2
+    x, y, z = lax.rem(chip, 2), lax.rem(chip // 2, 2), chip // 4
+    tokens = acts.shape[0]
+    width = slabs.shape[2]
+    chunks = width // kc
+    out_chunks = half_out // kc
+    half_in = width - half_out
+    chips = 4 * nz
+
+    def dev(i):
+        return {"blk": i}
+
+    def place(cx, cy, cz, cc):
+        return cz * 8 + cy * 4 + cx * 2 + cc
+
+    sibling = place(x, y, z, 1 - core)
+    to_x = place(1 - x, y, z, core)
+    to_y = place(x, 1 - y, z, core)
+    to_up = place(x, y, jnp.minimum(z + 1, nz - 1), core)
+    to_down = place(x, y, jnp.maximum(z - 1, 0), core)
+
+    local = [
+        pltpu.make_async_copy(slabs, buf.at[chip], own_sem.at[0]),
+        pltpu.make_async_copy(grads.at[:, :half_out], tok_l.at[:tokens, :half_out], own_sem.at[1]),
+        pltpu.make_async_copy(grads.at[:, half_out:], tok_r.at[:tokens, :half_out], own_sem.at[2]),
+        pltpu.make_async_copy(acts.at[:, :half_in], tok_l.at[:tokens, half_out:], own_sem.at[3]),
+        pltpu.make_async_copy(acts.at[:, half_in:], tok_r.at[:tokens, half_out:], own_sem.at[4]),
+    ]
+    for copy in local:
+        copy.start()
+
+    barrier = pltpu.get_barrier_semaphore()
+    for k in range(1, 8):
+        pl.semaphore_signal(barrier, inc=1, device_id=dev(z * 8 + lax.rem(lax.rem(me, 8) + k, 8)), device_id_type=MESH)
+    for k in range(1, nz):
+        pl.semaphore_signal(barrier, inc=1, device_id=dev(lax.rem(me + 8 * k, 8 * nz)), device_id_type=MESH)
+    pl.semaphore_wait(barrier, 7 + nz - 1)
+
+    acc[...] = jnp.zeros_like(acc)
+    local[0].wait()
+
+    def ids_copy():
+        return pltpu.make_async_remote_copy(
+            src_ref=ids, dst_ref=ids2, send_sem=ids_sem.at[0], recv_sem=ids_sem.at[1],
+            device_id=dev(sibling), device_id_type=MESH)
+
+    def token_copies(c, kind):
+        source, half, base = ((grads, half_out, 0), (acts, half_in, half_out))[kind]
+        at = pl.multiple_of(c * kc, LANES)
+        rel = pl.multiple_of(at - base, LANES)
+        other = pl.multiple_of(rel + half, LANES)
+        return [
+            pltpu.make_async_remote_copy(
+                src_ref=source.at[:, pl.ds(begin, kc)],
+                dst_ref=tok.at[pl.ds(tokens, tokens), pl.ds(at, kc)],
+                send_sem=tok_send.at[side, c], recv_sem=tok_sem.at[side, c],
+                device_id=dev(sibling), device_id_type=MESH)
+            for side, (begin, tok) in enumerate(((rel, tok_l), (other, tok_r)))
+        ]
+
+    def start_tokens(c):
+        for kind, test in ((0, c < out_chunks), (1, c >= out_chunks)):
+            @pl.when(test)
+            def _():
+                for copy in token_copies(c, kind):
+                    copy.start()
+
+    def piece(s, c, way, target):
+        view = buf.at[s, :, :, pl.ds(pl.multiple_of(c * kc, LANES), kc)]
+        return pltpu.make_async_remote_copy(
+            src_ref=view, dst_ref=view, send_sem=send_sem.at[way, c], recv_sem=recv_sem.at[s, c],
+            device_id=dev(target), device_id_type=MESH)
+
+    def is_plane_first(c):
+        k = lax.rem(c, 9)
+        return jnp.logical_or(k == 3, k == 7)
+
+    def event(zs, pos, t):
+        gap = jnp.abs(z - zs)
+        hops = gap + (0, 1, 1, 2)[pos]
+        c = t - LAG * hops
+        sx, sy = (x, 1 - x, x, 1 - x)[pos], (y, y, 1 - y, 1 - y)[pos]
+        s = zs * 4 + sy * 2 + sx
+
+        @pl.when(jnp.logical_and(c >= 0, c < chunks))
+        def _():
+            if pos == 0:
+                @pl.when(gap > 0)
+                def _():
+                    piece(s, c, 0, to_x).wait_recv()
+            else:
+                piece(s, c, 0, to_x).wait_recv()
+            plane_first = is_plane_first(c)
+            odd = lax.rem(zs + c, 2) == 1
+            along = plane_first if pos else jnp.bool_(True)
+            flat = jnp.logical_or(jnp.logical_not(plane_first), gap == 0)
+
+            @pl.when(along & (z >= zs) & (z < nz - 1))
+            def _():
+                piece(s, c, 2, to_up).start()
+
+            @pl.when(along & (z <= zs) & (z > 0))
+            def _():
+                piece(s, c, 3, to_down).start()
+
+            if pos in (0, 2):
+                @pl.when(flat if pos == 0 else flat & odd)
+                def _():
+                    piece(s, c, 0, to_x).start()
+            if pos in (0, 1):
+                @pl.when(flat if pos == 0 else flat & jnp.logical_not(odd))
+                def _():
+                    piece(s, c, 1, to_y).start()
+
+    def multiply(c):
+        cols = pl.ds(pl.multiple_of(c * kc, LANES), kc)
+        kind = jnp.where(c >= out_chunks, 1, 0)
+        for side, tok in ((0, tok_l), (1, tok_r)):
+            pltpu.make_async_copy(
+                tok.at[pl.ds(tokens, tokens), cols], tok.at[pl.ds(tokens, tokens), cols], tok_sem.at[side, c]
+            ).wait()
+        rest = buf[:, 2, :, cols].reshape(chips * SUB, kc)
+        for side, tok in ((0, tok_l), (1, tok_r)):
+            rows = jnp.concatenate([buf[:, side, :, cols].reshape(chips * SUB, kc), rest], axis=0)
+            acc[kind, side] += lax.dot_general(
+                tok[:, cols], rows, (((1,), (1,)), ((), ())), preferred_element_type=jnp.float32)
+
+    last = LAG * (nz - 1 + DEPTH_PLANE)
+    ids_copy().start()
+
+    @pl.loop(0, chunks + last)
+    def _(t):
+        for zs in range(nz):
+            event(zs, 0, t)
+        for pos in (1, 2, 3):
+            for zs in range(nz):
+                event(zs, pos, t)
+
+        @pl.when(t < chunks)
+        def _():
+            start_tokens(t)
+
+        @pl.when(t == last)
+        def _():
+            for copy in local[1:]:
+                copy.wait()
+
+        @pl.when(t >= last)
+        def _():
+            multiply(t - last)
+
+    n_main = chips * SUB
+    def joined(kind):
+        left, right = acc[kind, 0], acc[kind, 1]
+        main = left[:, :n_main] + right[:, :n_main]
+        tail = left[:, n_main:] + pltpu.roll(right[:, n_main:], n_main - SUB // 2, 1)
+        return jnp.concatenate([main, tail], axis=1)
+
+    scores = jnp.dot(joined(0) * joined(1), owner[...], precision=lax.Precision.HIGHEST,
+                     preferred_element_type=jnp.float32)
+    part[...] = scores[tokens:]
+    back = pltpu.make_async_remote_copy(
+        src_ref=part, dst_ref=part_in, send_sem=back_sem.at[0], recv_sem=back_sem.at[1],
+        device_id=dev(sibling), device_id_type=MESH)
+    back.start()
+    ids_copy().wait()
+    seq_rows = sums.shape[0]
+    lane = lax.broadcasted_iota(jnp.int32, (tokens, LANES), 1)
+    mine = jnp.where(lane == QUERIES, 1.0, scores[:tokens])
+    row = lax.broadcasted_iota(jnp.int32, (seq_rows, tokens), 0)
+
+    def by_sequence(which, values):
+        member = (row == which[...]).astype(jnp.float32)
+        return jnp.dot(member, values, precision=lax.Precision.HIGHEST, preferred_element_type=jnp.float32)
+
+    sums[...] = by_sequence(ids, mine) + by_sequence(ids2, scores[tokens:])
+    spot = lax.rem(me, 8)
+
+    def plane_copy(k):
+        return pltpu.make_async_remote_copy(
+            src_ref=sums, dst_ref=plane_in.at[k - 1], send_sem=plane_sem.at[0, k - 1], recv_sem=plane_sem.at[1, k - 1],
+            device_id=dev(z * 8 + lax.rem(spot + k, 8)), device_id_type=MESH)
+
+    for k in range(1, 8):
+        plane_copy(k).start()
+    back.wait()
+    ts_out[...] = scores[:tokens] + part_in[...]
+    for k in range(1, 8):
+        plane_copy(k).wait()
+    total = jnp.zeros((seq_rows, LANES), jnp.float32)
+    own = sums[...]
+    held = [own] + [plane_in[k - 1] for k in range(1, 8)]
+    for i in range(8):
+        k = lax.rem(spot - i + 8, 8)
+        term = jnp.zeros_like(total)
+        for j in range(8):
+            term = jnp.where(k == j, held[j], term)
+        total = total + term
+    line[...] = total
+
+    def line_copy(k):
+        return pltpu.make_async_remote_copy(
+            src_ref=line, dst_ref=line_in.at[k - 1], send_sem=line_sem.at[0, k - 1], recv_sem=line_sem.at[1, k - 1],
+            device_id=dev(lax.rem(me + 8 * k, 8 * nz)), device_id_type=MESH)
+
+    for k in range(1, nz):
+        line_copy(k).start()
+    for k in range(1, nz):
+        line_copy(k).wait()
+    held = [total] + [line_in[k - 1] for k in range(1, nz)]
+    total = jnp.zeros_like(total)
+    for i in range(nz):
+        k = lax.rem(z - i + nz, nz)
+        term = jnp.zeros_like(total)
+        for j in range(nz):
+            term = jnp.where(k == j, held[j], term)
+        total = total + term
+    seq_out[...] = total / jnp.sqrt(total[:, QUERIES:QUERIES + 1])
+
+    def sent(way, c, n):
+        view = buf.at[pl.ds(0, n), :, :, pl.ds(0, kc)]
+        pltpu.make_async_remote_copy(
+            src_ref=view, dst_ref=view, send_sem=send_sem.at[way, c], recv_sem=recv_sem.at[0, 0],
+            device_id=dev(to_x), device_id_type=MESH).wait_send()
+
+    @pl.loop(0, chunks)
+    def _(c):
+        plane_first = is_plane_first(c)
+        for kind, test in ((0, jnp.logical_not(plane_first)), (1, plane_first)):
+            for odd_c in (0, 1):
+                n_odd = sum((zs + odd_c) % 2 for zs in range(nz))
+
+                @pl.when(test & (lax.rem(c, 2) == odd_c))
+                def _():
+                    if kind == 0:
+                        sent(0, c, nz + n_odd)
+                        sent(1, c, nz + nz - n_odd)
+                    else:
+                        for own_odd in (0, 1):
+                            @pl.when(lax.rem(z, 2) == own_odd)
+                            def _():
+                                n = (own_odd + odd_c) % 2
+                                sent(0, c, 1 + n)
+                                sent(1, c, 2 - n)
+            for k in range(nz):
+                @pl.when(test & (z == k))
+                def _():
+                    each = 4 if kind else 1
+                    if k < nz - 1:
+                        sent(2, c, each * (k + 1))
+                    if k > 0:
+                        sent(3, c, each * (nz - k))
+        for kind, test in ((0, c < out_chunks), (1, c >= out_chunks)):
+            @pl.when(test)
+            def _():
+                for copy in token_copies(c, kind):
+                    copy.wait_send()
+
+
+def routed(nz):
+    def run(activations, out_grads, query_factors, pair_query, segment_ids):
+        n = lax.axis_size("blk")
+        chips = n // 2
+        core = lax.rem(lax.axis_index("blk"), 2)
+        rows = query_factors.shape[0]
+        tokens, wide = out_grads.shape
+        narrow = activations.shape[1]
+        half_out, half_in = wide // 2, narrow // 2
+        width = half_out + half_in
+        seqs = 2 * tokens * n // SEQ_LEN
+        left = jnp.concatenate([query_factors[:, :half_out], query_factors[:, wide:wide + half_in]], axis=1)
+        right = jnp.concatenate([query_factors[:, half_out:wide], query_factors[:, wide + half_in:]], axis=1)
+        slabs = jnp.stack([left[:SUB], right[:SUB], jnp.concatenate([left[SUB:], right[SUB:]], axis=0)])
+        mine = lax.dynamic_index_in_dim(pair_query.reshape(chips, 2, rows), core, axis=1, keepdims=False)
+        tail = jnp.pad(mine[:, SUB:], ((0, 0), (0, 2 * SUB - rows)), constant_values=-1)
+        which = jnp.concatenate([mine[:, :SUB].reshape(-1), tail.reshape(-1)])
+        owner = (which[:, None] == jnp.arange(LANES, dtype=jnp.int32)[None, :]).astype(jnp.float32)
+        seq_rows = -(-seqs // SUB) * SUB
+        chunks = width // CHUNK
+        vmem, any_ = pl.BlockSpec(memory_space=pltpu.VMEM), pl.BlockSpec(memory_space=pl.ANY)
+        f32 = jnp.float32
+        dma = pltpu.SemaphoreType.DMA
+        scores, seq = pl.pallas_call(
+            lambda *refs: kernel(nz, CHUNK, seqs, half_out, *refs),
+            name="routed_scores",
+            out_shape=(jax.ShapeDtypeStruct((tokens, LANES), f32), jax.ShapeDtypeStruct((seq_rows, LANES), f32)),
+            in_specs=[any_, any_, any_, vmem, vmem],
+            out_specs=(vmem, vmem),
+            scratch_shapes=[
+                pltpu.VMEM((chips, 3, SUB, width), jnp.bfloat16),
+                pltpu.VMEM((2 * tokens, width), jnp.bfloat16),
+                pltpu.VMEM((2 * tokens, width), jnp.bfloat16),
+                pltpu.VMEM((2, 2, 2 * tokens, 2 * chips * SUB), f32),
+                pltpu.VMEM((1, tokens), jnp.int32),
+                pltpu.VMEM((tokens, LANES), f32),
+                pltpu.VMEM((tokens, LANES), f32),
+                pltpu.VMEM((seq_rows, LANES), f32),
+                pltpu.VMEM((7, seq_rows, LANES), f32),
+                pltpu.VMEM((seq_rows, LANES), f32),
+                pltpu.VMEM((nz - 1, seq_rows, LANES), f32),
+                dma((chips, chunks)),
+                dma((4, chunks)),
+                dma((2, chunks)),
+                dma((2, chunks)),
+                dma((5,)),
+                dma((2,)),
+                dma((2,)),
+                dma((2, 7)),
+                dma((2, nz - 1)),
+            ],
+            compiler_params=pltpu.CompilerParams(
+                collective_id=0, has_side_effects=True, vmem_limit_bytes=60 * 1024 * 1024),
+        )(slabs, activations, out_grads, segment_ids.reshape(1, -1), owner)
+        return scores[:, :QUERIES], seq[:seqs, :QUERIES]
+
+    return run
+
+
 def solution(mesh):
+    nz = depth_of(mesh)
     in_specs = (
         P(("grp", "blk"), None),
         P(("grp", "blk"), None),
@@ -60,4 +407,4 @@
         P(("grp", "blk")),
     )
     out_specs = (P(("grp", "blk"), None), P("grp", None))
-    return jax.shard_map(local, mesh=mesh, in_specs=in_specs, out_specs=out_specs, check_vma=False)
+    return jax.shard_map(routed(nz) if nz > 1 else local, mesh=mesh, in_specs=in_specs, out_specs=out_specs, check_vma=False)

time: 308 us -> 132 us (0.43)
  waiting for transfers between devices: 215 us -> 0 us
  Pallas kernels: 0 us -> 124 us
  blocking collectives: 38.3 us -> 0 us
  matrix products: 21.6 us -> 0 us
  between operations: 14.1 us -> 0.7 us
  local copies, waits for them, and re-layouts: 16.1 us -> 5.37 us
    all_gather x1 -> x0, waiting for transfers between devices: 214 us -> none  [local(): lax.all_gather(query_factors, 'blk', axis=0, tiled=True, axis_index_group...]
    pallas_call x0 -> x1, Pallas kernels: none -> 124 us  [run(): pl.pallas_call(lambda *refs: kernel(nz, CHUNK, seqs, half_out, *refs), na...]
    psum x1 -> x0, blocking collectives: 38.3 us -> none  [local(): totals, counts = lax.psum((partial_sums, partial_counts), 'blk')]
    dot_general x7 -> x0, matrix products: 21.6 us -> none  [the longest x2 15.4 us: pair_products(): lax.dot_general(out_grads, piece[:, :width], numbers, preferred_element_t...]
    unnamed x7 -> x3, local copies, waits for them, and re-layouts: 15.2 us -> 1.52 us
    slice x0 -> x4, local copies, waits for them, and re-layouts: none -> 3.54 us  [the longest x1 1.26 us: run(): return (scores[:, :QUERIES], seq[:seqs, :QUERIES])]
  transfers between devices with their start and end apart: 4 -> 0, of which waited for: 1 -> 0; matrix products, arithmetic and copies ran while one was open for 10% -> 0% of each run, Pallas kernels for 0% -> 0%
where the time goes in v2:
time: 132 us
  Pallas kernels  124 us (94%)
  local copies, waits for them, and re-layouts  5.37 us (4%)
  other arithmetic  1.97 us (1%)
    pallas_call x1, Pallas kernels, run(): pl.pallas_call(lambda *refs: kernel(nz, CHUNK, seqs, half_out, *refs), na...  124 us

profile of v2, /device:TPU:0, one launch (start us, length us, event | category | flops | bytes accessed | tf_op | source)
XLA Modules:
  0.0 131.7 jit_solution(5031820064854448630)
XLA Ops:
  0.6 1.2 fusion.10
  1.9 1.0 fusion.11
  2.8 0.2 fusion.5
  3.0 0.0 copy-start
  3.1 1.0 pad_maximum_fusion.refs_0_
  4.1 0.0 copy-done
  4.1 0.1 reshape.18
  4.2 0.1 slice.53
  4.3 0.1 reshape.20
  4.4 0.1 reshape.19
  4.5 0.8 fusion.9.refs_4_
  5.3 123.7 %routed_scores.1 = (f32[128,128]{1,0:T(8,128)}, f32[8,128]{1,0:T(8,128)}) custom-call(bf16[3,8,18432]{2,1,0:T(8,128)(2,1)} %pad_maximum_fusion.refs_0_, bf16[128,8192]{1,0:T(8,128)(2,1)} %refs_1_.1, bf16[128,28672]{1,0:T(8,128)(2,1)} %refs_2_.1, s32[1,128]{1,0:T(1,128)} %bitcast.13, f32[256,128]{1,0:T(8,128)} %fusion.9.refs_4_), custom_call_target="tpu_custom_call" | custom-call | tf_op jit(solution)/shard_map/routed_scores/pallas_call | solution.py:364
  129.0 1.5 %copy.8 = f32[128,12]{0,1:T(8,128)} copy(f32[128,12]{1,0:T(8,128)} %bitcast.12) | data formatting | bytes 12288
  130.5 1.3 slice.47
  (3 shorter events, 0.0 us)
Async XLA Ops:
  3.0 1.0 copy-start

commit v3 on v2

--- a/solution.py
+++ b/solution.py
@@ -57,7 +57,9 @@
 SUB = 8
 LANES = 128
 CHUNK = 1024
-LAG = 2
+LAG = 3
+AHEAD = 5
+PLANE_FIRST = (1, 5)
 DEPTH_PLANE = 2
 
 
@@ -74,7 +76,7 @@
     return sizes["blk"] // 8
 
 
-def kernel(nz, kc, seqs, half_out, slabs, acts, grads, ids, owner, ts_out, seq_out,
+def kernel(nz, kc, seqs, half_out, factors, tail, acts, grads, ids, owner, ts_out, seq_out,
            buf, tok_l, tok_r, acc, ids2, part, part_in, sums, plane_in, line, line_in,
            recv_sem, send_sem, tok_sem, tok_send, own_sem, ids_sem, back_sem, plane_sem, line_sem):
     me = lax.axis_index("blk")
@@ -82,7 +84,7 @@
     chip = me // 2
     x, y, z = lax.rem(chip, 2), lax.rem(chip // 2, 2), chip // 4
     tokens = acts.shape[0]
-    width = slabs.shape[2]
+    width = tail.shape[1]
     chunks = width // kc
     out_chunks = half_out // kc
     half_in = width - half_out
@@ -101,13 +103,20 @@
     to_down = place(x, y, jnp.maximum(z - 1, 0), core)
 
     local = [
-        pltpu.make_async_copy(slabs, buf.at[chip], own_sem.at[0]),
-        pltpu.make_async_copy(grads.at[:, :half_out], tok_l.at[:tokens, :half_out], own_sem.at[1]),
-        pltpu.make_async_copy(grads.at[:, half_out:], tok_r.at[:tokens, :half_out], own_sem.at[2]),
-        pltpu.make_async_copy(acts.at[:, :half_in], tok_l.at[:tokens, half_out:], own_sem.at[3]),
-        pltpu.make_async_copy(acts.at[:, half_in:], tok_r.at[:tokens, half_out:], own_sem.at[4]),
+        pltpu.make_async_copy(grads.at[:, :half_out], tok_l.at[:tokens, :half_out], own_sem.at[5]),
+        pltpu.make_async_copy(grads.at[:, half_out:], tok_r.at[:tokens, :half_out], own_sem.at[6]),
+        pltpu.make_async_copy(acts.at[:, :half_in], tok_l.at[:tokens, half_out:], own_sem.at[7]),
+        pltpu.make_async_copy(acts.at[:, half_in:], tok_r.at[:tokens, half_out:], own_sem.at[8]),
     ]
-    for copy in local:
+    wide = 2 * half_out
+    factor_copies = [pltpu.make_async_copy(tail, buf.at[chip, 2], own_sem.at[0])]
+    for side in (0, 1):
+        for k, (begin, at, size) in enumerate((
+            (side * half_out, 0, half_out), (wide + side * half_in, half_out, half_in))):
+            factor_copies.append(pltpu.make_async_copy(
+                factors.at[:SUB, begin:begin + size], buf.at[chip, side, :, at:at + size],
+                own_sem.at[1 + 2 * side + k]))
+    for copy in factor_copies + local:
         copy.start()
 
     barrier = pltpu.get_barrier_semaphore()
@@ -118,7 +127,8 @@
     pl.semaphore_wait(barrier, 7 + nz - 1)
 
     acc[...] = jnp.zeros_like(acc)
-    local[0].wait()
+    for copy in factor_copies:
+        copy.wait()
 
     def ids_copy():
         return pltpu.make_async_remote_copy(
@@ -154,12 +164,17 @@
 
     def is_plane_first(c):
         k = lax.rem(c, 9)
-        return jnp.logical_or(k == 3, k == 7)
+        hit = jnp.bool_(False)
+        for at in PLANE_FIRST:
+            hit = hit | (k == at)
+        return hit
 
     def event(zs, pos, t):
         gap = jnp.abs(z - zs)
         hops = gap + (0, 1, 1, 2)[pos]
         c = t - LAG * hops
+        if pos == 0:
+            c = jnp.where(gap == 0, c + AHEAD, c)
         sx, sy = (x, 1 - x, x, 1 - x)[pos], (y, y, 1 - y, 1 - y)[pos]
         s = zs * 4 + sy * 2 + sx
 
@@ -209,21 +224,22 @@
     last = LAG * (nz - 1 + DEPTH_PLANE)
     ids_copy().start()
 
-    @pl.loop(0, chunks + last)
-    def _(t):
+    @pl.loop(0, chunks + last + AHEAD)
+    def _(step):
+        t = step - AHEAD
         for zs in range(nz):
             event(zs, 0, t)
         for pos in (1, 2, 3):
             for zs in range(nz):
                 event(zs, pos, t)
 
-        @pl.when(t < chunks)
+        @pl.when((t >= 0) & (t < chunks))
         def _():
             start_tokens(t)
 
         @pl.when(t == last)
         def _():
-            for copy in local[1:]:
+            for copy in local:
                 copy.wait()
 
         @pl.when(t >= last)
@@ -265,7 +281,7 @@
     for k in range(1, 8):
         plane_copy(k).start()
     back.wait()
-    ts_out[...] = scores[:tokens] + part_in[...]
+    ts_out[...] = jnp.transpose(scores[:tokens] + part_in[...])[:QUERIES]
     for k in range(1, 8):
         plane_copy(k).wait()
     total = jnp.zeros((seq_rows, LANES), jnp.float32)
@@ -296,7 +312,7 @@
         for j in range(nz):
             term = jnp.where(k == j, held[j], term)
         total = total + term
-    seq_out[...] = total / jnp.sqrt(total[:, QUERIES:QUERIES + 1])
+    seq_out[...] = (total / jnp.sqrt(total[:, QUERIES:QUERIES + 1]))[:seqs, :QUERIES]
 
     def sent(way, c, n):
         view = buf.at[pl.ds(0, n), :, :, pl.ds(0, kc)]
@@ -349,9 +365,10 @@
         half_out, half_in = wide // 2, narrow // 2
         width = half_out + half_in
         seqs = 2 * tokens * n // SEQ_LEN
-        left = jnp.concatenate([query_factors[:, :half_out], query_factors[:, wide:wide + half_in]], axis=1)
-        right = jnp.concatenate([query_factors[:, half_out:wide], query_factors[:, wide + half_in:]], axis=1)
-        slabs = jnp.stack([left[:SUB], right[:SUB], jnp.concatenate([left[SUB:], right[SUB:]], axis=0)])
+        low = query_factors[SUB:]
+        left = jnp.concatenate([low[:, :half_out], low[:, wide:wide + half_in]], axis=1)
+        right = jnp.concatenate([low[:, half_out:wide], low[:, wide + half_in:]], axis=1)
+        rest = jnp.concatenate([left, right], axis=0)
         mine = lax.dynamic_index_in_dim(pair_query.reshape(chips, 2, rows), core, axis=1, keepdims=False)
         tail = jnp.pad(mine[:, SUB:], ((0, 0), (0, 2 * SUB - rows)), constant_values=-1)
         which = jnp.concatenate([mine[:, :SUB].reshape(-1), tail.reshape(-1)])
@@ -364,8 +381,8 @@
         scores, seq = pl.pallas_call(
             lambda *refs: kernel(nz, CHUNK, seqs, half_out, *refs),
             name="routed_scores",
-            out_shape=(jax.ShapeDtypeStruct((tokens, LANES), f32), jax.ShapeDtypeStruct((seq_rows, LANES), f32)),
-            in_specs=[any_, any_, any_, vmem, vmem],
+            out_shape=(jax.ShapeDtypeStruct((QUERIES, tokens), f32), jax.ShapeDtypeStruct((seqs, QUERIES), f32)),
+            in_specs=[any_, any_, any_, any_, vmem, vmem],
             out_specs=(vmem, vmem),
             scratch_shapes=[
                 pltpu.VMEM((chips, 3, SUB, width), jnp.bfloat16),
@@ -383,7 +400,7 @@
                 dma((4, chunks)),
                 dma((2, chunks)),
                 dma((2, chunks)),
-                dma((5,)),
+                dma((9,)),
                 dma((2,)),
                 dma((2,)),
                 dma((2, 7)),
@@ -391,8 +408,8 @@
             ],
             compiler_params=pltpu.CompilerParams(
                 collective_id=0, has_side_effects=True, vmem_limit_bytes=60 * 1024 * 1024),
-        )(slabs, activations, out_grads, segment_ids.reshape(1, -1), owner)
-        return scores[:, :QUERIES], seq[:seqs, :QUERIES]
+        )(query_factors, rest, activations, out_grads, segment_ids.reshape(1, -1), owner)
+        return scores.T, seq
 
     return run
 

time: 132 us -> 128 us (0.970)
  Pallas kernels: 124 us -> 121 us
    pallas_call x1, Pallas kernels: 124 us -> 121 us  [run(): pl.pallas_call(lambda *refs: kernel(nz, CHUNK, seqs, half_out, *refs), na...]
    slice x3 -> x2, local copies, waits for them, and re-layouts: 3.47 us -> 2.01 us  [the longest x1 1.11 us: run(): low[:, :half_out]]
where the time goes in v3:
time: 128 us
  Pallas kernels  121 us (95%)
  local copies, waits for them, and re-layouts  4.94 us (4%)
  other arithmetic  1.61 us (1%)
    pallas_call x1, Pallas kernels, run(): pl.pallas_call(lambda *refs: kernel(nz, CHUNK, seqs, half_out, *refs), na...  121 us

profile of v3, /device:TPU:0, one launch (start us, length us, event | category | flops | bytes accessed | tf_op | source)
XLA Modules:
  0.0 128.0 jit_solution(12062452609039252760)
XLA Ops:
  0.6 0.0 copy-start
  0.6 0.9 fusion.2
  1.5 1.1 fusion.1
  2.7 0.9 maximum_maximum_fusion.refs_1_
  3.5 0.0 copy-done
  3.5 0.1 reshape.18
  3.7 0.1 slice.30
  3.7 0.1 reshape.20
  3.8 0.1 reshape.19
  3.9 0.7 fusion.refs_5_
  4.7 120.7 %routed_scores.1 = (f32[12,128]{1,0:T(8,128)}, f32[4,12]{1,0:T(4,128)}) custom-call(bf16[12,36864]{1,0:T(8,128)(2,1)} %refs_0_.1, bf16[8,18432]{1,0:T(8,128)(2,1)} %maximum_maximum_fusion.refs_1_, bf16[128,8192]{1,0:T(8,128)(2,1)} %refs_2_.1, bf16[128,28672]{1,0:T(8,128)(2,1)} %refs_3_.1, s32[1,128]{1,0:T(1,128)} %bitcast.7, f32[256,128]{1,0:T(8,128)} %fusion.refs_5_), custom_call_target="tpu_custom_call" | custom-call | tf_op jit(solution)/shard_map/routed_scores/pallas_call | solution.py:381
  125.4 1.3 %copy.9 = f32[128,12]{0,1:T(8,128)} copy(f32[128,12]{0,1:T(8,128)} %bitcast.6) | data formatting | bytes 12288
  126.7 1.2 copy.10
  (3 shorter events, 0.0 us)
Async XLA Ops:
  0.6 2.9 %copy-start = (s32[384]{0:T(512)S(1)}, s32[384]{0:T(512)}, u32[]{:S(2)}) copy-start(s32[384]{0:T(512)} %param.8) | copy-start | bytes 4612
